TPU v7x, 32 devices: a whole 2x2x4 slice. The times are simulated.
32 devices in a mesh: groups: 2 (over x), docs: 16 (over z, y, core).
Axes of the slice: x: 2, y: 2, z: 4, core: 2. Of those that a mesh axis runs over, the one named last changes fastest.
Arguments:
- embeddings: bfloat16 [4096, 1024], P(('groups', 'docs')), parts along dimension 0, may hold values from -100 to 100
- labels: int32 [4096], P(('groups', 'docs')), parts along dimension 0, may hold values from 0 to 15, as said below
- row_slot: int32 [4096], P(('groups', 'docs')), parts along dimension 0, may hold values from 0 to 2047, as said below
Outputs:
- density: float32 [4096], P(('groups', 'docs')), parts along dimension 0
- neighbour_mean: bfloat16 [4096, 1024], P(('groups', 'docs')), parts along dimension 0
There are 2 independent parts, one for each index of `groups`. A program takes and returns all parts, laid end to end along the dimension named above; each array names one. Nothing has to cross between parts.
Inputs may be any that keep to these rules, and one draw needn't show every extreme that they name: row_slot is a permutation of 0 to 2047; at most 16 documents of one device take rows of one block, and some device places exactly 16 documents in some block. All documents in one block share one label; documents with equal labels lie in blocks at most 3 apart, and some label spans 4 blocks.
All inputs are finite; a program needn't handle non-finite values.
Results may differ from a plain program's by a relative error of at most 0.0029.
Values may be sent and summed in bfloat16 or wider, within the bound.
A program may use at most 64 MiB of HBM per device.

v0:
```python
import math

import jax
import jax.numpy as jnp
from jax import lax
from jax.sharding import PartitionSpec as P

REACH = 3


neg_large = -1e30
kernel_gain = 4.0


def from_behind(block, axis, distance):
    devices = range(lax.axis_size(axis))
    route = [(i - distance, i) for i in devices if i - distance in devices]
    return lax.ppermute(block, axis, route)


def side_terms(scores, same_label, values):
    masked = jnp.where(same_label, scores, neg_large)
    row_max = jnp.max(masked, axis=1)
    weights = jnp.where(same_label, jnp.exp(masked - row_max[:, None]), 0.0)
    row_total = jnp.sum(weights, axis=1)
    rounded = weights.astype(jnp.bfloat16)
    row_accum = jnp.dot(rounded, values, preferred_element_type=jnp.float32)
    return (row_max, row_total, row_accum)


def block_terms(own_x, own_tag, far_x, far_tag, exclude_self, both_sides):
    feature_width = own_x.shape[1]
    scores = jnp.dot(own_x, far_x.T, preferred_element_type=jnp.float32) * (
        kernel_gain / math.sqrt(feature_width)
    )
    same_label = own_tag[:, None] == far_tag[None, :]
    if exclude_self:
        positions = jnp.arange(own_x.shape[0], dtype=jnp.int32)
        same_label = same_label & (positions[:, None] != positions[None, :])
    own_side = side_terms(scores, same_label, far_x)
    if both_sides:
        far_side = side_terms(scores.T, same_label.T, own_x)
        return (own_side, far_side)
    return own_side


def combine(first_terms, second_terms):
    row_max = jnp.maximum(first_terms[0], second_terms[0])
    scale_first = jnp.exp(first_terms[0] - row_max)
    scale_second = jnp.exp(second_terms[0] - row_max)
    row_total = first_terms[1] * scale_first + second_terms[1] * scale_second
    row_accum = first_terms[2] * scale_first[:, None] + second_terms[2] * scale_second[:, None]
    return (row_max, row_total, row_accum)


def per_device(embeddings, labels, row_slot):
    device_count = lax.axis_size("docs")
    my_index = lax.axis_index("docs")
    row_count = embeddings.shape[0]
    feature_width = embeddings.shape[1]
    capacity = max(2, 2 * row_count // device_count)
    target_block = row_slot // row_count
    same_target = target_block[:, None] == target_block[None, :]
    earlier = lax.broadcasted_iota(jnp.int32, (row_count, row_count), 1) < lax.broadcasted_iota(
        jnp.int32, (row_count, row_count), 0
    )
    slot_rank = jnp.sum((same_target & earlier).astype(jnp.int32), axis=1)
    where_sent = target_block * capacity + slot_rank
    label_tag = (labels + 1).astype(jnp.bfloat16)
    out_x = (
        jnp.zeros((device_count * capacity, feature_width), jnp.bfloat16)
        .at[where_sent]
        .set(embeddings)
    )
    out_tag = jnp.zeros((device_count * capacity,), jnp.bfloat16).at[where_sent].set(label_tag)
    out_slot = jnp.full((device_count * capacity,), -1, jnp.int32).at[where_sent].set(row_slot)
    got_x, got_tag = (
        lax.all_to_all(
            out_x.reshape(device_count, capacity, feature_width),
            "docs",
            split_axis=0,
            concat_axis=0,
            tiled=True,
        ),
        lax.all_to_all(
            out_tag.reshape(device_count, capacity), "docs", split_axis=0, concat_axis=0, tiled=True
        ),
    )
    got_slot = lax.all_to_all(
        out_slot.reshape(device_count, capacity), "docs", split_axis=0, concat_axis=0, tiled=True
    )
    local_row = jnp.where(got_slot >= 0, got_slot % row_count, row_count).reshape(-1)
    block_x = (
        jnp.zeros((row_count, feature_width), jnp.bfloat16)
        .at[local_row]
        .set(got_x.reshape(-1, feature_width), mode="drop")
    )
    block_tag = (
        jnp.zeros((row_count,), jnp.bfloat16).at[local_row].set(got_tag.reshape(-1), mode="drop")
    )
    nothing = (
        jnp.full((row_count,), neg_large, jnp.float32),
        jnp.zeros((row_count,), jnp.float32),
        jnp.zeros((row_count, feature_width), jnp.float32),
    )
    running = block_terms(block_x, block_tag, block_x, block_tag, True, False)

    def pair_both(far_block, far_labels):
        return block_terms(block_x, block_tag, far_block, far_labels, False, True)

    def pair_none(far_block, far_labels):
        return (nothing, nothing)

    for distance in range(1, REACH + 1):
        far_block, far_labels = from_behind((block_x, block_tag), "docs", -distance)
        has_pairs = jnp.any(block_tag[:, None] == far_labels[None, :])
        own_side, far_side = lax.cond(has_pairs, pair_both, pair_none, far_block, far_labels)
        running = combine(running, own_side)
        received = from_behind(far_side, "docs", distance)
        received = (
            jnp.where(my_index >= distance, received[0], neg_large),
            received[1],
            received[2],
        )
        running = combine(running, received)
    row_max, row_total, row_accum = running
    density_block = row_max + jnp.log(row_total)
    mean_block = (row_accum / row_total[:, None]).astype(jnp.bfloat16)
    holder = jnp.clip(local_row, 0, row_count - 1)
    back_mean = mean_block[holder].reshape(device_count, capacity, feature_width)
    back_density = density_block[holder].reshape(device_count, capacity)
    home_mean = lax.all_to_all(back_mean, "docs", split_axis=0, concat_axis=0, tiled=True)
    home_density = lax.all_to_all(back_density, "docs", split_axis=0, concat_axis=0, tiled=True)
    mean_rows = home_mean.reshape(-1, feature_width)[where_sent]
    density_rows = home_density.reshape(-1)[where_sent]
    return (density_rows, mean_rows)


def solution(mesh):
    return jax.shard_map(
        per_device,
        mesh=mesh,
        in_specs=(P(("groups", "docs"), None), P(("groups", "docs")), P(("groups", "docs"))),
        out_specs=(P(("groups", "docs")), P(("groups", "docs"), None)),
        check_vma=False,
    )
```

profile of v0, /device:TPU:1, one launch (start us, length us, event | category | flops | bytes accessed | tf_op | source)
XLA Modules:
  0.0 139.1 jit_solution(11661431307159607264)
XLA Ops:
  0.6 0.7 and_select_fusion.1
  1.5 0.5 copy-done.19
  2.0 1.3 scatter_custom_fusion.1
  3.3 0.7 all_to_all.35
  4.0 7.3 %all-to-all-start.1 = ((bf16[16,1,16]{2,1,0:T(2,128)(2,1)}), bf16[16,1,16]{2,1,0:T(2,128)(2,1)S(1)}, u32[]{:S(2)}, u32[]{:S(2)}) async-start(bf16[16,1,16]{2,1,0:T(2,128)(2,1)} %all_to_all.35), calls=%async_computation.1 | async-start | bytes 16384 | tf_op jit(solution)/shard_map/all_to_all | solution.py:85
  11.4 1.0 scatter_custom_fusion
  12.3 0.7 all_to_all.26
  13.0 4.1 %all-to-all-done.1 = bf16[16,1,16]{2,1,0:T(2,128)(2,1)S(1)} async-done(((bf16[16,1,16]{2,1,0:T(2,128)(2,1)}), bf16[16,1,16]{2,1,0:T(2,128)(2,1)S(1)}, u32[]{:S(2)}, u32[]{:S(2)}) %all-to-all-start.1) | async-done | bytes 544 | tf_op jit(solution)/shard_map/all_to_all | solution.py:85
  17.2 4.0 %all-to-all-start = ((s32[16,1,16]{2,1,0:T(1,128)}), s32[16,1,16]{2,1,0:T(1,128)S(1)}, u32[]{:S(2)}, u32[]{:S(2)}) async-start(s32[16,1,16]{2,1,0:T(1,128)} %all_to_all.26), calls=%async_computation | async-start | bytes 16384 | tf_op jit(solution)/shard_map/all_to_all | solution.py:89
  21.2 2.4 %scatter_custom_fusion.3 = bf16[256,1024]{1,0:T(8,128)(2,1)} fusion(s32[128]{0:T(128)S(1)} %get-tuple-element.112, bf16[128,1024]{1,0:T(8,128)(2,1)} %param.9, bf16[]{:T(256)} %constant.30.clone.1), kind=kCustom, calls=%fused_computation.94 | custom fusion | bytes 524800 | tf_op jit(solution)/shard_map/scatter | solution.py:73
  23.5 3.4 %all-to-all-done = s32[16,1,16]{2,1,0:T(1,128)S(1)} async-done(((s32[16,1,16]{2,1,0:T(1,128)}), s32[16,1,16]{2,1,0:T(1,128)S(1)}, u32[]{:S(2)}, u32[]{:S(2)}) %all-to-all-start) | async-done | bytes 1056 | tf_op jit(solution)/shard_map/all_to_all | solution.py:89
  27.0 4.1 %all-to-all-start.2 = ((bf16[16,16,1024]{2,1,0:T(8,128)(2,1)}), bf16[16,16,1024]{2,1,0:T(8,128)(2,1)S(1)}, u32[]{:S(2)}, u32[]{:S(2)}) async-start(bf16[16,16,1024]{2,1,0:T(8,128)(2,1)} %bitcast.4), calls=%async_computation.2 | async-start | bytes 1048576 | tf_op jit(solution)/shard_map/all_to_all | solution.py:78
  31.2 0.5 broadcast.233
  31.7 0.7 reduce.7
  32.5 2.2 %scatter_custom_fusion.2 = bf16[128]{0:T(256)(128)(2,1)S(1)} fusion(s32[256]{0:T(256)S(1)} %bitcast.57, bf16[256]{0:T(256)(128)(2,1)S(1)} %reshape.227, bf16[]{:T(256)} %constant.30.clone.1), kind=kCustom, calls=%fused_computation.149 | custom fusion | bytes 258 | tf_op jit(solution)/shard_map/scatter | solution.py:99
  34.7 2.1 %collective-permute-start = (bf16[128]{0:T(256)(128)(2,1)S(1)}, bf16[128]{0:T(256)(128)(2,1)S(1)}, u32[]{:S(2)}, u32[]{:S(2)}) collective-permute-start(bf16[128]{0:T(256)(128)(2,1)S(1)} %scatter_custom_fusion.2), channel_id=1, source_target_pairs={{1,0},{2,1},{3,2},{4,3},{5,4},{6,5},{7,6},{8,7},{9,8},{10,9},{11,1... | collective-permute-start | bytes 776 | tf_op jit(solution)/shard_map/ppermute | solution.py:18
  36.8 1.3 collective-permute-start.3
  38.1 1.3 collective-permute-start.6
  39.4 0.4 collective-permute-done
  39.8 1.6 %collective-permute-done.3 = bf16[128]{0:T(256)(128)(2,1)S(1)} collective-permute-done((bf16[128]{0:T(256)(128)(2,1)S(1)}, bf16[128]{0:T(256)(128)(2,1)S(1)}, u32[]{:S(2)}, u32[]{:S(2)}) %collective-permute-start.3) | collective-permute-done | bytes 288 | tf_op jit(solution)/shard_map/ppermute | solution.py:18
  41.5 3.6 %collective-permute-done.6 = bf16[128]{0:T(256)(128)(2,1)S(1)} collective-permute-done((bf16[128]{0:T(256)(128)(2,1)S(1)}, bf16[128]{0:T(256)(128)(2,1)S(1)}, u32[]{:S(2)}, u32[]{:S(2)}) %collective-permute-start.6) | collective-permute-done | bytes 288 | tf_op jit(solution)/shard_map/ppermute | solution.py:18
  45.1 0.8 compare_reduce_fusion.1
  47.9 1.7 %scatter_custom_fusion.4 = bf16[128,1024]{1,0:T(8,128)(2,1)S(1)} fusion(s32[256]{0:T(256)S(1)} %bitcast.58, bf16[256,1024]{1,0:T(8,128)(2,1)S(1)} %bitcast.55, bf16[]{:T(256)} %constant.30.clone.1), kind=kCustom, calls=%fused_computation.96 | custom fusion | bytes 262146 | tf_op jit(solution)/shard_map/scatter | solution.py:96
  49.6 1.9 %collective-permute-start.1 = (bf16[128,1024]{1,0:T(8,128)(2,1)S(1)}, bf16[128,1024]{1,0:T(8,128)(2,1)S(1)}, u32[]{:S(2)}, u32[]{:S(2)}) collective-permute-start(bf16[128,1024]{1,0:T(8,128)(2,1)S(1)} %scatter_custom_fusion.4), channel_id=1, source_target_pairs={{1,0},{2,1},{3,2},{4,3},{5,4},{6,5},{7,6},{8,7},{9,8},{10,9},{11,1... | collective-permute-start | bytes 786440 | tf_op jit(solution)/shard_map/ppermute | solution.py:18
  51.5 1.3 collective-permute-start.4
  52.8 1.3 collective-permute-start.7
  54.5 4.3 %collective-permute-done.1 = bf16[128,1024]{1,0:T(8,128)(2,1)S(1)} collective-permute-done((bf16[128,1024]{1,0:T(8,128)(2,1)S(1)}, bf16[128,1024]{1,0:T(8,128)(2,1)S(1)}, u32[]{:S(2)}, u32[]{:S(2)}) %collective-permute-start.1) | collective-permute-done | bytes 262176 | tf_op jit(solution)/shard_map/ppermute | solution.py:18
  58.7 2.7 %conditional.3 = (f32[128]{0:T(128)S(1)}, f32[128]{0:T(128)S(1)}, f32[128,1024]{1,0:T(8,128)S(1)}, f32[128]{0:T(128)S(1)}, f32[128]{0:T(128)S(1)}, /*index=5*/f32[128,1024]{1,0:T(8,128)}) conditional(s32[]{:T(128)} %convert_element_type.41, () %tuple.32, (bf16[128]{0:T(256)(128)(2,1)S(1)}, bf16[128]{0:T(256)(128)(2,1)S(1)}, ...), branch_computations={%region_8.9_spmd, %region_9.14_spmd} | conditional | flops 101105152 | bytes 2701472 | solution.py:117
  59.2 1.1 fusion.6
  60.3 0.3 fusion.8
  60.8 0.6 copy-done.1
  61.5 1.9 %collective-permute-start.2 = (f32[128]{0:T(128)S(1)}, f32[128]{0:T(128)S(1)}, u32[]{:S(2)}, u32[]{:S(2)}) collective-permute-start(f32[128]{0:T(128)S(1)} %get-tuple-element.57), channel_id=1, source_target_pairs={{0,1},{1,2},{2,3},{3,4},{4,5},{5,6},{6,7},{7,8},{8,9},{9,10},{10,1... | collective-permute-start | bytes 1544 | tf_op jit(solution)/shard_map/ppermute | solution.py:18
  63.4 2.8 %conditional.4 = (f32[128]{0:T(128)S(1)}, f32[128]{0:T(128)S(1)}, f32[128,1024]{1,0:T(8,128)S(1)}, f32[128]{0:T(128)S(1)}, f32[128]{0:T(128)S(1)}, /*index=5*/f32[128,1024]{1,0:T(8,128)}) conditional(s32[]{:T(128)} %convert_element_type.42, () %tuple.34, (bf16[128]{0:T(256)(128)(2,1)S(1)}, bf16[128]{0:T(256)(128)(2,1)S(1)}, ...), branch_computations={%region_15.16_spmd, %region_16.21_spmd} | conditional | flops 101105152 | bytes 2701472 | solution.py:117
  63.9 1.1 fusion.30
  65.5 0.6 copy-done.3
  66.2 1.9 %collective-permute-start.5 = (f32[128]{0:T(128)S(1)}, f32[128]{0:T(128)S(1)}, u32[]{:S(2)}, u32[]{:S(2)}) collective-permute-start(f32[128]{0:T(128)S(1)} %get-tuple-element.59), channel_id=1, source_target_pairs={{0,2},{1,3},{2,4},{3,5},{4,6},{5,7},{6,8},{7,9},{8,10},{9,11},{10,... | collective-permute-start | bytes 1544 | tf_op jit(solution)/shard_map/ppermute | solution.py:18
  68.1 4.7 %collective-permute-start.10 = (f32[128]{0:T(128)S(1)}, f32[128]{0:T(128)S(1)}, u32[]{:S(2)}, u32[]{:S(2)}) collective-permute-start(f32[128]{0:T(128)S(1)} %get-tuple-element.65), channel_id=1, source_target_pairs={{0,2},{1,3},{2,4},{3,5},{4,6},{5,7},{6,8},{7,9},{8,10},{9,11},{10,... | collective-permute-start | bytes 1544 | tf_op jit(solution)/shard_map/ppermute | solution.py:18
  72.8 3.7 %collective-permute-start.9 = (f32[128]{0:T(128)S(1)}, f32[128]{0:T(128)S(1)}, u32[]{:S(2)}, u32[]{:S(2)}) collective-permute-start(f32[128]{0:T(128)S(1)} %get-tuple-element.63), channel_id=1, source_target_pairs={{0,1},{1,2},{2,3},{3,4},{4,5},{5,6},{6,7},{7,8},{8,9},{9,10},{10,1... | collective-permute-start | bytes 1544 | tf_op jit(solution)/shard_map/ppermute | solution.py:18
  76.5 1.0 conditional.5
  76.6 0.9 broadcast_in_dim.74.clone
  77.5 0.5 copy-done.27
  78.0 5.2 %collective-permute-start.11 = (f32[128]{0:T(128)S(1)}, f32[128]{0:T(128)S(1)}, u32[]{:S(2)}, u32[]{:S(2)}) collective-permute-start(f32[128]{0:T(128)S(1)} %get-tuple-element.67), channel_id=1, source_target_pairs={{0,3},{1,4},{2,5},{3,6},{4,7},{5,8},{6,9},{7,10},{8,11},{9,12},{10... | collective-permute-start | bytes 1544 | tf_op jit(solution)/shard_map/ppermute | solution.py:18
  83.3 1.9 %collective-permute-start.8 = (f32[128]{0:T(128)S(1)}, f32[128]{0:T(128)S(1)}, u32[]{:S(2)}, u32[]{:S(2)}) collective-permute-start(f32[128]{0:T(128)S(1)} %get-tuple-element.61), channel_id=1, source_target_pairs={{0,3},{1,4},{2,5},{3,6},{4,7},{5,8},{6,9},{7,10},{8,11},{9,12},{10... | collective-permute-start | bytes 1544 | tf_op jit(solution)/shard_map/ppermute | solution.py:18
  85.2 3.2 %collective-permute-start.12 = (f32[128,1024]{1,0:T(8,128)}, f32[128,1024]{1,0:T(8,128)S(1)}, u32[]{:S(2)}, u32[]{:S(2)}) collective-permute-start(f32[128,1024]{1,0:T(8,128)} %get-tuple-element.69), channel_id=1, source_target_pairs={{0,1},{1,2},{2,3},{3,4},{4,5},{5,6},{6,7},{7,8},{8,9},{9,10},{10,1... | collective-permute-start | bytes 1572872 | tf_op jit(solution)/shard_map/ppermute | solution.py:18
  88.4 0.5 copy-done.21
  89.0 1.8 %collective-permute-start.13 = (f32[128,1024]{1,0:T(8,128)}, f32[128,1024]{1,0:T(8,128)S(1)}, u32[]{:S(2)}, u32[]{:S(2)}) collective-permute-start(f32[128,1024]{1,0:T(8,128)} %get-tuple-element.71), channel_id=1, source_target_pairs={{0,2},{1,3},{2,4},{3,5},{4,6},{5,7},{6,8},{7,9},{8,10},{9,11},{10,... | collective-permute-start | bytes 1572872 | tf_op jit(solution)/shard_map/ppermute | solution.py:18
  90.8 0.6 copy-done.23
  91.4 1.3 collective-permute-start.14
  92.8 0.6 copy-done.24
  93.5 1.2 log_add_fusion
  94.7 1.9 %gather_fusion = f32[256]{0:T(256)S(1)} fusion(f32[128]{0:T(128)S(1)} %get-tuple-element.91, s32[1024]{0:T(1024)S(1)} %pad_clamp_fusion.1), kind=kCustom, calls=%fused_computation | custom fusion | bytes 3072 | tf_op jit(solution)/shard_map/gather | solution.py:131
  96.6 0.7 all_to_all.32
  97.3 4.3 %all-to-all-start.3 = ((f32[16,1,16]{2,1,0:T(1,128)}), f32[16,1,16]{2,1,0:T(1,128)S(1)}, u32[]{:S(2)}, u32[]{:S(2)}) async-start(f32[16,1,16]{2,1,0:T(1,128)} %all_to_all.32), calls=%async_computation.3 | async-start | bytes 16384 | tf_op jit(solution)/shard_map/all_to_all | solution.py:133
  101.5 0.6 copy-done.18
  102.2 0.3 convolution_multiply_fusion.3
  102.5 6.2 %collective-permute-done.13 = f32[128,1024]{1,0:T(8,128)S(1)} collective-permute-done((f32[128,1024]{1,0:T(8,128)}, f32[128,1024]{1,0:T(8,128)S(1)}, u32[]{:S(2)}, u32[]{:S(2)}) %collective-permute-start.13) | collective-permute-done | bytes 524320 | tf_op jit(solution)/shard_map/ppermute | solution.py:18
  108.8 0.4 divide_convert_fusion
  109.2 2.0 %gather_fusion.2 = bf16[256,1024]{1,0:T(8,128)(2,1)} fusion(bf16[128,1024]{1,0:T(8,128)(2,1)S(1)} %divide_convert_fusion, s32[1024]{0:T(1024)S(1)} %pad_clamp_fusion.1), kind=kCustom, calls=%fused_computation.2 | custom fusion | bytes 1049600 | tf_op jit(solution)/shard_map/gather | solution.py:130
  111.1 12.4 %all-to-all-start.4 = ((bf16[16,16,1024]{2,1,0:T(8,128)(2,1)}), bf16[16,16,1024]{2,1,0:T(8,128)(2,1)S(1)}, u32[]{:S(2)}, u32[]{:S(2)}) async-start(bf16[16,16,1024]{2,1,0:T(8,128)(2,1)} %bitcast.7), calls=%async_computation.4 | async-start | bytes 1048576 | tf_op jit(solution)/shard_map/all_to_all | solution.py:132
  123.6 0.5 broadcast.234
  124.1 0.7 reduce.8
  124.9 1.8 %gather_fusion.1 = f32[128]{0:T(128)} fusion(f32[256]{0:T(256)S(1)} %reshape.172, s32[1024]{0:T(1024)S(1)} %pad_clamp_fusion), kind=kCustom, calls=%fused_computation.1 | custom fusion | bytes 1536 | tf_op jit(solution)/shard_map/gather | solution.py:135
  126.6 10.9 %all-to-all-done.4 = bf16[16,16,1024]{2,1,0:T(8,128)(2,1)S(1)} async-done(((bf16[16,16,1024]{2,1,0:T(8,128)(2,1)}), bf16[16,16,1024]{2,1,0:T(8,128)(2,1)S(1)}, u32[]{:S(2)}, u32[]{:S(2)}) %all-to-all-start.4) | async-done | bytes 524320 | tf_op jit(solution)/shard_map/all_to_all | solution.py:132
  137.6 1.6 %gather_fusion.3 = bf16[128,1024]{1,0:T(8,128)(2,1)} fusion(bf16[256,1024]{1,0:T(8,128)(2,1)S(1)} %bitcast.54, s32[1024]{0:T(1024)S(1)} %pad_clamp_fusion), kind=kCustom, calls=%fused_computation.3 | custom fusion | bytes 524800 | tf_op jit(solution)/shard_map/gather | solution.py:134
  (81 shorter events, 2.5 us)
Async XLA Ops:
  1.3 0.7 copy-start.19
  1.3 0.7 copy-start.20
  2.0 19.2 %copy-start.12 = (s32[128]{0:T(128)}, s32[128]{0:T(128)S(1)}, u32[]{:S(2)}) copy-start(s32[128]{0:T(128)S(1)} %get-tuple-element.112) | copy-start | bytes 1540
  4.0 13.2 %all-to-all-start.1 = ((bf16[16,1,16]{2,1,0:T(2,128)(2,1)}), bf16[16,1,16]{2,1,0:T(2,128)(2,1)S(1)}, u32[]{:S(2)}, u32[]{:S(2)}) async-start(bf16[16,1,16]{2,1,0:T(2,128)(2,1)} %all_to_all.35), calls=%async_computation.1 | async-start | bytes 16384 | tf_op jit(solution)/shard_map/all_to_all | solution.py:85
  17.2 9.8 %all-to-all-start = ((s32[16,1,16]{2,1,0:T(1,128)}), s32[16,1,16]{2,1,0:T(1,128)S(1)}, u32[]{:S(2)}, u32[]{:S(2)}) async-start(s32[16,1,16]{2,1,0:T(1,128)} %all_to_all.26), calls=%async_computation | async-start | bytes 16384 | tf_op jit(solution)/shard_map/all_to_all | solution.py:89
  27.0 20.9 %all-to-all-start.2 = ((bf16[16,16,1024]{2,1,0:T(8,128)(2,1)}), bf16[16,16,1024]{2,1,0:T(8,128)(2,1)S(1)}, u32[]{:S(2)}, u32[]{:S(2)}) async-start(bf16[16,16,1024]{2,1,0:T(8,128)(2,1)} %bitcast.4), calls=%async_computation.2 | async-start | bytes 1048576 | tf_op jit(solution)/shard_map/all_to_all | solution.py:78
  34.7 5.2 %collective-permute-start = (bf16[128]{0:T(256)(128)(2,1)S(1)}, bf16[128]{0:T(256)(128)(2,1)S(1)}, u32[]{:S(2)}, u32[]{:S(2)}) collective-permute-start(bf16[128]{0:T(256)(128)(2,1)S(1)} %scatter_custom_fusion.2), channel_id=1, source_target_pairs={{1,0},{2,1},{3,2},{4,3},{5,4},{6,5},{7,6},{8,7},{9,8},{10,9},{11,1... | collective-permute-start | bytes 776 | tf_op jit(solution)/shard_map/ppermute | solution.py:18
  36.8 4.7 %collective-permute-start.3 = (bf16[128]{0:T(256)(128)(2,1)S(1)}, bf16[128]{0:T(256)(128)(2,1)S(1)}, u32[]{:S(2)}, u32[]{:S(2)}) collective-permute-start(bf16[128]{0:T(256)(128)(2,1)S(1)} %scatter_custom_fusion.2), channel_id=1, source_target_pairs={{2,0},{3,1},{4,2},{5,3},{6,4},{7,5},{8,6},{9,7},{10,8},{11,9},{12,... | collective-permute-start | bytes 776 | tf_op jit(solution)/shard_map/ppermute | solution.py:18
  38.1 7.0 %collective-permute-start.6 = (bf16[128]{0:T(256)(128)(2,1)S(1)}, bf16[128]{0:T(256)(128)(2,1)S(1)}, u32[]{:S(2)}, u32[]{:S(2)}) collective-permute-start(bf16[128]{0:T(256)(128)(2,1)S(1)} %scatter_custom_fusion.2), channel_id=1, source_target_pairs={{3,0},{4,1},{5,2},{6,3},{7,4},{8,5},{9,6},{10,7},{11,8},{12,9},{13... | collective-permute-start | bytes 776 | tf_op jit(solution)/shard_map/ppermute | solution.py:18
  49.6 9.1 %collective-permute-start.1 = (bf16[128,1024]{1,0:T(8,128)(2,1)S(1)}, bf16[128,1024]{1,0:T(8,128)(2,1)S(1)}, u32[]{:S(2)}, u32[]{:S(2)}) collective-permute-start(bf16[128,1024]{1,0:T(8,128)(2,1)S(1)} %scatter_custom_fusion.4), channel_id=1, source_target_pairs={{1,0},{2,1},{3,2},{4,3},{5,4},{6,5},{7,6},{8,7},{9,8},{10,9},{11,1... | collective-permute-start | bytes 786440 | tf_op jit(solution)/shard_map/ppermute | solution.py:18
  51.5 11.9 %collective-permute-start.4 = (bf16[128,1024]{1,0:T(8,128)(2,1)S(1)}, bf16[128,1024]{1,0:T(8,128)(2,1)S(1)}, u32[]{:S(2)}, u32[]{:S(2)}) collective-permute-start(bf16[128,1024]{1,0:T(8,128)(2,1)S(1)} %scatter_custom_fusion.4), channel_id=1, source_target_pairs={{2,0},{3,1},{4,2},{5,3},{6,4},{7,5},{8,6},{9,7},{10,8},{11,9},{12,... | collective-permute-start | bytes 786440 | tf_op jit(solution)/shard_map/ppermute | solution.py:18
  52.8 23.7 %collective-permute-start.7 = (bf16[128,1024]{1,0:T(8,128)(2,1)S(1)}, bf16[128,1024]{1,0:T(8,128)(2,1)S(1)}, u32[]{:S(2)}, u32[]{:S(2)}) collective-permute-start(bf16[128,1024]{1,0:T(8,128)(2,1)S(1)} %scatter_custom_fusion.4), channel_id=1, source_target_pairs={{3,0},{4,1},{5,2},{6,3},{7,4},{8,5},{9,6},{10,7},{11,8},{12,9},{13... | collective-permute-start | bytes 786440 | tf_op jit(solution)/shard_map/ppermute | solution.py:18
  59.2 1.5 %copy-start = (f32[128]{0:T(128)}, f32[128]{0:T(128)S(1)}, u32[]{:S(2)}) copy-start(f32[128]{0:T(128)S(1)} %get-tuple-element.144) | copy-start | bytes 1540 | tf_op jit(solution)/shard_map/cond
  59.2 1.5 %copy-start.6 = (f32[128]{0:T(128)}, f32[128]{0:T(128)S(1)}, u32[]{:S(2)}) copy-start(f32[128]{0:T(128)S(1)} %get-tuple-element.147) | copy-start | bytes 1540 | tf_op jit(solution)/shard_map/cond
  60.8 0.7 copy-start.1
  60.8 0.6 copy-start.7
  61.5 1.9 %copy-start.25 = (f32[128]{0:T(128)}, f32[128]{0:T(128)S(1)}, u32[]{:S(2)}) copy-start(f32[128]{0:T(128)S(1)} %get-tuple-element.62) | copy-start | bytes 1540
  61.5 21.8 %collective-permute-start.2 = (f32[128]{0:T(128)S(1)}, f32[128]{0:T(128)S(1)}, u32[]{:S(2)}, u32[]{:S(2)}) collective-permute-start(f32[128]{0:T(128)S(1)} %get-tuple-element.57), channel_id=1, source_target_pairs={{0,1},{1,2},{2,3},{3,4},{4,5},{5,6},{6,7},{7,8},{8,9},{9,10},{10,1... | collective-permute-start | bytes 1544 | tf_op jit(solution)/shard_map/ppermute | solution.py:18
  63.9 1.5 %copy-start.2 = (f32[128]{0:T(128)}, f32[128]{0:T(128)S(1)}, u32[]{:S(2)}) copy-start(f32[128]{0:T(128)S(1)} %get-tuple-element.132) | copy-start | bytes 1540 | tf_op jit(solution)/shard_map/cond
  63.9 1.5 %copy-start.8 = (f32[128]{0:T(128)}, f32[128]{0:T(128)S(1)}, u32[]{:S(2)}) copy-start(f32[128]{0:T(128)S(1)} %get-tuple-element.135) | copy-start | bytes 1540 | tf_op jit(solution)/shard_map/cond
  65.5 0.7 copy-start.3
  65.5 0.6 copy-start.9
  66.2 1.9 %copy-start.26 = (f32[128]{0:T(128)}, f32[128]{0:T(128)S(1)}, u32[]{:S(2)}) copy-start(f32[128]{0:T(128)S(1)} %get-tuple-element.64) | copy-start | bytes 1540
  66.2 19.0 %collective-permute-start.5 = (f32[128]{0:T(128)S(1)}, f32[128]{0:T(128)S(1)}, u32[]{:S(2)}, u32[]{:S(2)}) collective-permute-start(f32[128]{0:T(128)S(1)} %get-tuple-element.59), channel_id=1, source_target_pairs={{0,2},{1,3},{2,4},{3,5},{4,6},{5,7},{6,8},{7,9},{8,10},{9,11},{10,... | collective-permute-start | bytes 1544 | tf_op jit(solution)/shard_map/ppermute | solution.py:18
  68.1 20.3 %collective-permute-start.10 = (f32[128]{0:T(128)S(1)}, f32[128]{0:T(128)S(1)}, u32[]{:S(2)}, u32[]{:S(2)}) collective-permute-start(f32[128]{0:T(128)S(1)} %get-tuple-element.65), channel_id=1, source_target_pairs={{0,2},{1,3},{2,4},{3,5},{4,6},{5,7},{6,8},{7,9},{8,10},{9,11},{10,... | collective-permute-start | bytes 1544 | tf_op jit(solution)/shard_map/ppermute | solution.py:18
  72.8 18.0 %collective-permute-start.9 = (f32[128]{0:T(128)S(1)}, f32[128]{0:T(128)S(1)}, u32[]{:S(2)}, u32[]{:S(2)}) collective-permute-start(f32[128]{0:T(128)S(1)} %get-tuple-element.63), channel_id=1, source_target_pairs={{0,1},{1,2},{2,3},{3,4},{4,5},{5,6},{6,7},{7,8},{8,9},{9,10},{10,1... | collective-permute-start | bytes 1544 | tf_op jit(solution)/shard_map/ppermute | solution.py:18
  77.5 0.5 copy-start.27
  78.0 14.7 %collective-permute-start.11 = (f32[128]{0:T(128)S(1)}, f32[128]{0:T(128)S(1)}, u32[]{:S(2)}, u32[]{:S(2)}) collective-permute-start(f32[128]{0:T(128)S(1)} %get-tuple-element.67), channel_id=1, source_target_pairs={{0,3},{1,4},{2,5},{3,6},{4,7},{5,8},{6,9},{7,10},{8,11},{9,12},{10... | collective-permute-start | bytes 1544 | tf_op jit(solution)/shard_map/ppermute | solution.py:18
  83.2 9.5 %copy-start.14 = (f32[128]{0:T(128)}, f32[128]{0:T(128)S(1)}, u32[]{:S(2)}) copy-start(f32[128]{0:T(128)S(1)} %collective-permute-done.2) | copy-start | bytes 1540
  83.3 9.5 %collective-permute-start.8 = (f32[128]{0:T(128)S(1)}, f32[128]{0:T(128)S(1)}, u32[]{:S(2)}, u32[]{:S(2)}) collective-permute-start(f32[128]{0:T(128)S(1)} %get-tuple-element.61), channel_id=1, source_target_pairs={{0,3},{1,4},{2,5},{3,6},{4,7},{5,8},{6,9},{7,10},{8,11},{9,12},{10... | collective-permute-start | bytes 1544 | tf_op jit(solution)/shard_map/ppermute | solution.py:18
  85.2 7.5 %copy-start.16 = (f32[128]{0:T(128)}, f32[128]{0:T(128)S(1)}, u32[]{:S(2)}) copy-start(f32[128]{0:T(128)S(1)} %collective-permute-done.5) | copy-start | bytes 1540
  85.2 17.3 %collective-permute-start.12 = (f32[128,1024]{1,0:T(8,128)}, f32[128,1024]{1,0:T(8,128)S(1)}, u32[]{:S(2)}, u32[]{:S(2)}) collective-permute-start(f32[128,1024]{1,0:T(8,128)} %get-tuple-element.69), channel_id=1, source_target_pairs={{0,1},{1,2},{2,3},{3,4},{4,5},{5,6},{6,7},{7,8},{8,9},{9,10},{10,1... | collective-permute-start | bytes 1572872 | tf_op jit(solution)/shard_map/ppermute | solution.py:18
  88.4 0.5 copy-start.21
  89.0 19.8 %collective-permute-start.13 = (f32[128,1024]{1,0:T(8,128)}, f32[128,1024]{1,0:T(8,128)S(1)}, u32[]{:S(2)}, u32[]{:S(2)}) collective-permute-start(f32[128,1024]{1,0:T(8,128)} %get-tuple-element.71), channel_id=1, source_target_pairs={{0,2},{1,3},{2,4},{3,5},{4,6},{5,7},{6,8},{7,9},{8,10},{9,11},{10,... | collective-permute-start | bytes 1572872 | tf_op jit(solution)/shard_map/ppermute | solution.py:18
  90.8 0.6 copy-start.23
  91.4 17.4 %collective-permute-start.14 = (f32[128,1024]{1,0:T(8,128)}, f32[128,1024]{1,0:T(8,128)S(1)}, u32[]{:S(2)}, u32[]{:S(2)}) collective-permute-start(f32[128,1024]{1,0:T(8,128)} %get-tuple-element.73), channel_id=1, source_target_pairs={{0,3},{1,4},{2,5},{3,6},{4,7},{5,8},{6,9},{7,10},{8,11},{9,12},{10... | collective-permute-start | bytes 1572872 | tf_op jit(solution)/shard_map/ppermute | solution.py:18
  92.8 0.7 copy-start.24
  92.8 0.7 copy-start.28
  92.8 0.7 copy-start.15
  92.8 0.7 copy-start.17
  92.8 0.7 copy-start.22
  97.3 13.9 %all-to-all-start.3 = ((f32[16,1,16]{2,1,0:T(1,128)}), f32[16,1,16]{2,1,0:T(1,128)S(1)}, u32[]{:S(2)}, u32[]{:S(2)}) async-start(f32[16,1,16]{2,1,0:T(1,128)} %all_to_all.32), calls=%async_computation.3 | async-start | bytes 16384 | tf_op jit(solution)/shard_map/all_to_all | solution.py:133
  101.5 0.7 copy-start.18
  111.1 12.4 %copy-start.13 = (s32[128]{0:T(128)S(1)}, s32[128]{0:T(128)}, u32[]{:S(2)}) copy-start(s32[128]{0:T(128)} %copy-done.12) | copy-start | bytes 1540
  111.1 26.4 %all-to-all-start.4 = ((bf16[16,16,1024]{2,1,0:T(8,128)(2,1)}), bf16[16,16,1024]{2,1,0:T(8,128)(2,1)S(1)}, u32[]{:S(2)}, u32[]{:S(2)}) async-start(bf16[16,16,1024]{2,1,0:T(8,128)(2,1)} %bitcast.7), calls=%async_computation.4 | async-start | bytes 1048576 | tf_op jit(solution)/shard_map/all_to_all | solution.py:132
where the time goes:
time: 139 us
  starting transfers between devices  67 us (48%)
  waiting for transfers between devices  34.8 us (25%)
  local copies, waits for them, and re-layouts  24.9 us (18%)
  other arithmetic  5.32 us (4%)
  matrix products  3.93 us (3%)
  between operations  3.03 us (2%)
    ppermute x15, starting transfers between devices, from_behind(): return lax.ppermute(block, axis, route)  34.9 us
    ppermute x15, waiting for transfers between devices, from_behind(): return lax.ppermute(block, axis, route)  16.2 us
    all_to_all x1, starting transfers between devices, per_device(): lax.all_to_all(back_mean, 'docs', split_axis=0, concat_axis=0, tiled=True)  12.4 us
    all_to_all x1, waiting for transfers between devices, per_device(): lax.all_to_all(back_mean, 'docs', split_axis=0, concat_axis=0, tiled=True)  10.9 us
    all_to_all x1, starting transfers between devices, per_device(): lax.all_to_all(out_tag.reshape(device_count, capacity), 'docs', split_axi...  7.34 us
    all_to_all x1, starting transfers between devices, per_device(): lax.all_to_all(back_density, 'docs', split_axis=0, concat_axis=0, tiled=T...  4.25 us
    all_to_all x1, waiting for transfers between devices, per_device(): lax.all_to_all(out_tag.reshape(device_count, capacity), 'docs', split_axi...  4.14 us
    all_to_all x1, starting transfers between devices, per_device(): lax.all_to_all(out_x.reshape(device_count, capacity, feature_width), 'doc...  4.08 us
  transfers between devices with their start and end apart: 20, of which 8 were waited for; matrix products, arithmetic and copies ran while one was open for 16% of the time, Pallas kernels for 0%

commit v1 on v0

v1 whole, which is shorter than its diff:
```python
import math

import jax
import jax.numpy as jnp
from jax import lax
from jax.sharding import PartitionSpec as P

neg_large = -1e30
kernel_gain = 4.0


def per_device(embeddings, labels, row_slot):
    my_index = lax.axis_index("docs")
    row_count, feature_width = embeddings.shape
    all_x = lax.all_gather(embeddings, "docs", axis=0, tiled=True)
    all_labels = lax.all_gather(labels, "docs", axis=0, tiled=True)
    scores = jnp.dot(embeddings, all_x.T, preferred_element_type=jnp.float32) * (
        kernel_gain / math.sqrt(feature_width)
    )
    mine = my_index * row_count + jnp.arange(row_count, dtype=jnp.int32)
    every = jnp.arange(all_x.shape[0], dtype=jnp.int32)
    near = (labels[:, None] == all_labels[None, :]) & (mine[:, None] != every[None, :])
    masked = jnp.where(near, scores, neg_large)
    row_max = jnp.max(masked, axis=1)
    weights = jnp.where(near, jnp.exp(masked - row_max[:, None]), 0.0)
    row_total = jnp.sum(weights, axis=1)
    accum = jnp.dot(weights.astype(jnp.bfloat16), all_x, preferred_element_type=jnp.float32)
    return row_max + jnp.log(row_total), (accum / row_total[:, None]).astype(jnp.bfloat16)


def solution(mesh):
    return jax.shard_map(
        per_device,
        mesh=mesh,
        in_specs=(P(("groups", "docs"), None), P(("groups", "docs")), P(("groups", "docs"))),
        out_specs=(P(("groups", "docs")), P(("groups", "docs"), None)),
        check_vma=False,
    )
```

time: 139 us -> 77 us (0.55)
  starting transfers between devices: 67 us -> 0.04 us
  local copies, waits for them, and re-layouts: 24.9 us -> 0.01 us
  blocking collectives: 0 us -> 23.4 us
  between operations: 3.03 us -> 14 us
  other arithmetic: 5.32 us -> 0.98 us
  waiting for transfers between devices: 34.8 us -> 32.4 us
  matrix products: 3.93 us -> 5.77 us
    ppermute x15 -> x0, starting transfers between devices: 34.9 us -> none  [from_behind(): return lax.ppermute(block, axis, route)]
    all_to_all x5 -> x0, starting transfers between devices: 32.1 us -> none  [the longest x1 12.4 us: per_device(): lax.all_to_all(back_mean, 'docs', split_axis=0, concat_axis=0, tiled=True)]
    all_gather x0 -> x1, waiting for transfers between devices: none -> 31.7 us  [per_device(): all_x = lax.all_gather(embeddings, 'docs', axis=0, tiled=True)]
    all_gather x0 -> x1, blocking collectives: none -> 23.4 us  [per_device(): all_labels = lax.all_gather(labels, 'docs', axis=0, tiled=True)]
    all_to_all x5 -> x0, waiting for transfers between devices: 18.5 us -> none  [the longest x1 10.9 us: per_device(): lax.all_to_all(back_mean, 'docs', split_axis=0, concat_axis=0, tiled=True)]
    ppermute x15 -> x0, waiting for transfers between devices: 16.2 us -> none  [from_behind(): return lax.ppermute(block, axis, route)]
    scatter x5 -> x0, local copies, waits for them, and re-layouts: 8.54 us -> none  [the longest x1 2.37 us: per_device(): out_x = jnp.zeros((device_count * capacity, feature_width), jnp.bfloat16)...]
    gather x4 -> x0, local copies, waits for them, and re-layouts: 7.15 us -> none  [the longest x1 1.96 us: per_device(): mean_block[holder].reshape(device_count, capacity, feature_width)]
  transfers between devices with their start and end apart: 20 -> 1, of which waited for: 8 -> 1; matrix products, arithmetic and copies ran while one was open for 16% -> 0% of each run, Pallas kernels for 0% -> 0%
where the time goes in v1:
time: 77 us; the launch traced here: 76.6 us
  waiting for transfers between devices  32.4 us (42%)
  blocking collectives  23.4 us (30%)
  between operations  14 us (18%)
  matrix products  5.77 us (7%)
  other arithmetic  0.98 us (1%)
    all_gather x1, waiting for transfers between devices, per_device(): all_x = lax.all_gather(embeddings, 'docs', axis=0, tiled=True)  31.7 us
    all_gather x1, blocking collectives, per_device(): all_labels = lax.all_gather(labels, 'docs', axis=0, tiled=True)  23.4 us
    dot_general x1, matrix products, per_device(): jnp.dot(embeddings, all_x.T, preferred_element_type=jnp.float32)  4.03 us
    dot_general x1, matrix products, per_device(): jnp.dot(weights.astype(jnp.bfloat16), all_x, preferred_element_type=jnp.f...  1.74 us
  transfers between devices with their start and end apart: 1, of which 1 were waited for; matrix products, arithmetic and copies ran while one was open for 0% of the time, Pallas kernels for 0%

profile of v1, /device:TPU:1, one launch (start us, length us, event | category | flops | bytes accessed | tf_op | source)
XLA Modules:
  0.0 76.6 jit_solution(15819714501910202282)
XLA Ops:
  7.2 0.0 copy-start
  7.2 0.0 all-gather.3.cloned.1.call-start
  7.2 0.7 all-gather.3.cloned.1.call-update
  7.9 23.4 %all-gather = s32[16,1,128]{2,1,0:T(1,128)S(1)} all-gather(s32[1,1,128]{2,1,0:T(1,128)} %bitcast.8), channel_id=1, replica_groups=mesh['groups'=2,'docs'=16] {'docs'}, dimensions={0}, use_global_device_ids=true | all-gather | bytes 8704 | tf_op jit(solution)/shard_map/all_gather | solution.py:16
  31.3 31.7 %all-gather.3.cloned.1.call-done = bf16[2048,1024]{1,0:T(8,128)(2,1)} async-done(((bf16[128,1024]{1,0:T(8,128)(2,1)}), bf16[2048,1024]{1,0:T(8,128)(2,1)}) %all-gather.3.cloned.1.call-update) | async-done | bytes 4194320 | tf_op jit(solution)/shard_map/all_gather | solution.py:15
  63.0 0.0 copy-start.1
  63.0 4.0 %fusion.12 = (f32[128]{0:T(128)S(1)}, f32[128,2048]{1,0:T(8,128)S(1)}) fusion(bf16[128,1024]{1,0:T(8,128)(2,1)} %param.3, bf16[2048,1024]{1,0:T(8,128)(2,1)} %all-gather.3.cloned.1.call-done, s32[128]{0:T(128)S(1)} %iota_add_fusion, s32[2048]{0:T(1024)S(1)} %bitcast.5, s32[128]{0:T(128)} %param.4), kind=kOutput, calls=%fused_computation.17 | convolution fusion | flops 538443648 | bytes 5514752 | tf_op jit(solution)/shard_map/dot_general | solution.py:17
  67.1 0.0 copy-done
  67.1 0.4 fusion.4
  67.5 0.5 log_add_fusion
  68.1 0.0 copy-done.1
  68.1 1.7 %fusion.1 = bf16[128,1024]{1,0:T(8,128)(2,1)} fusion(bf16[2048,1024]{1,0:T(8,128)(2,1)S(1)} %copy-done.1, f32[128,2048]{1,0:T(8,128)S(1)} %get-tuple-element.3, f32[128]{0:T(128)S(1)} %get-tuple-element.2, s32[128]{0:T(128)S(1)} %iota_add_fusion, s32[2048]{0:T(1024)S(1)} %bitcast.7, s32[128]{0:T(128)S(1)} %copy-done, f32[128]{0:T(128)S(1)} %fusion.4), kind=kOutput, calls=%fused_computation.3 | convolution fusion | flops 538705920 | bytes 5515264 | tf_op jit(solution)/shard_map/dot_general | solution.py:27
  (1 shorter events, 0.0 us)
Async XLA Ops:
  7.2 59.9 %copy-start = (s32[128]{0:T(128)S(1)}, s32[128]{0:T(128)}, u32[]{:S(2)}) copy-start(s32[128]{0:T(128)} %param.4) | copy-start | bytes 1540
  7.2 55.9 %all-gather.3.cloned.1.call-start = ((), (), s32[]{:S(2)}) async-start(), calls=%async_computation | async-start | bytes 4456448 | tf_op jit(solution)/shard_map/all_gather | solution.py:15
  63.0 5.0 %copy-start.1 = (bf16[2048,1024]{1,0:T(8,128)(2,1)S(1)}, bf16[2048,1024]{1,0:T(8,128)(2,1)}, u32[]{:S(2)}) copy-start(bf16[2048,1024]{1,0:T(8,128)(2,1)} %all-gather.3.cloned.1.call-done) | copy-start | bytes 12582916
Sparse Core Ops, SparseCore 0:
  10.1 52.8 all-gather.2

commit v2 on v1

v2 whole, which is shorter than its diff:
```python
import functools
import math

import jax
import jax.numpy as jnp
from jax import lax
from jax.experimental import pallas as pl
from jax.experimental.pallas import tpu as pltpu
from jax.sharding import PartitionSpec as P

MESH = pl.DeviceIdType.MESH
CORES = 2
PIECES = 2

neg_large = -1e30
kernel_gain = 4.0


def chip_grid(device_count):
    chips = device_count // CORES
    fast = 1
    while (2 * fast) * (2 * fast) <= chips and chips % (2 * fast) == 0:
        fast *= 2
    return chips // fast, fast


def kernel(
    grid_slow, grid_fast, x_ref, lab_ref, dens_ref, mean_ref,
    buf, labs, acc, row_max, row_total, send_sem, recv_sem, lsend_sem, lrecv_sem, own_sem,
):
    rows, width = x_ref.shape
    part = rows // PIECES
    me = lax.axis_index("docs")
    core = lax.rem(me, CORES)
    chip = me // CORES
    y = lax.rem(chip, grid_fast)
    z = chip // grid_fast

    def device(zz, yy, cc):
        return (zz * grid_fast + yy) * CORES + cc

    targets = (
        (z > 0, device(z - 1, y, core)),
        (z < grid_slow - 1, device(z + 1, y, core)),
        (y > 0, device(z, y - 1, core)),
        (y < grid_fast - 1, device(z, y + 1, core)),
        (z >= 0, device(z, y, 1 - core)),
    )

    barrier = pltpu.get_barrier_semaphore()
    for there, target in targets:
        @pl.when(there)
        def _():
            pl.semaphore_signal(barrier, inc=1, device_id={"docs": target}, device_id_type=MESH)
    pl.semaphore_wait(barrier, sum(there.astype(jnp.int32) for there, _ in targets))

    def data_of(slot):
        return buf.at[pl.ds(pl.multiple_of(slot * part, part), part)]

    def copies(direction, zz, yy, piece, own):
        slot = device(zz, yy, core) * PIECES + piece
        sem = ((zz * grid_fast + yy) * PIECES) + piece
        target = {"docs": targets[direction][1]}
        data_src = x_ref.at[pl.ds(piece * part, part)] if own else data_of(slot)
        lab_src = lab_ref if own else labs.at[slot]
        return (
            pltpu.make_async_remote_copy(
                lab_src, labs.at[slot], lsend_sem.at[direction, sem], lrecv_sem.at[slot],
                device_id=target, device_id_type=MESH,
            ),
            pltpu.make_async_remote_copy(
                data_src, data_of(slot), send_sem.at[direction, sem], recv_sem.at[slot],
                device_id=target, device_id_type=MESH,
            ),
        )

    def each(directions, wanted, zz, yy, piece, own, act):
        for direction, want in zip(directions, wanted):
            @pl.when(jnp.logical_and(targets[direction][0], want))
            def _():
                for copy in copies(direction, zz, yy, piece, own):
                    act(copy)

    start = lambda copy: copy.start()
    finish = lambda copy: copy.wait_send()

    def arrived(zz, yy, cc, piece):
        slot = device(zz, yy, cc) * PIECES + piece
        for ref, send, recv in (
            (labs.at[slot], lsend_sem, lrecv_sem), (data_of(slot), send_sem, recv_sem)
        ):
            pltpu.make_async_remote_copy(
                ref, ref, send.at[0, 0], recv.at[slot],
                device_id={"docs": targets[4][1]}, device_id_type=MESH,
            ).wait_recv()

    yes = z >= 0
    for piece in range(PIECES):
        each((2, 3, 0, 1, 4), (yes,) * 5, z, y, piece, True, start)
    own_rows = buf.at[pl.ds(pl.multiple_of(me * rows, rows), rows)]
    own_copy = pltpu.make_async_copy(x_ref, own_rows, own_sem.at[0])
    own_copy.start()
    own_labs = labs.at[me * PIECES]
    own_lab_copy = pltpu.make_async_copy(lab_ref, own_labs, own_sem.at[1])
    own_lab_copy.start()

    row_max[...] = jnp.full_like(row_max, neg_large)
    row_total[...] = jnp.zeros_like(row_total)
    acc[...] = jnp.zeros_like(acc)
    label_column = jnp.transpose(
        jnp.broadcast_to(lab_ref[...].astype(jnp.float32), (rows, rows))
    )[:, :1]
    keys = CORES * rows
    gap = lax.broadcasted_iota(jnp.int32, (rows, keys), 1) - lax.broadcasted_iota(
        jnp.int32, (rows, keys), 0
    )
    own_copy.wait()
    own_lab_copy.wait()

    def compute(zz, yy):
        where = zz * grid_fast + yy
        values = buf[pl.ds(pl.multiple_of(where * keys, keys), keys), :]
        tags = jnp.concatenate(
            [labs[(where * CORES + cc) * PIECES] for cc in range(CORES)], axis=1
        ).astype(jnp.float32)
        scores = lax.dot_general(
            x_ref[...], values, (((1,), (1,)), ((), ())), preferred_element_type=jnp.float32
        ) * (kernel_gain / math.sqrt(width))
        self_gap = jnp.where(where == chip, core * rows, -keys)
        near = (label_column == tags) & (gap != self_gap)
        masked = jnp.where(near, scores, neg_large)
        before = row_max[...]
        peak = jnp.maximum(before, jnp.max(masked, axis=1, keepdims=True))
        weights = jnp.where(near, jnp.exp(masked - peak), 0.0)
        scale = jnp.exp(before - peak)
        row_max[...] = peak
        row_total[...] = row_total[...] * scale + jnp.sum(weights, axis=1, keepdims=True)
        acc[...] = acc[...] * scale + jnp.dot(
            weights.astype(jnp.bfloat16), values, preferred_element_type=jnp.float32
        )

    def visited(distance, side, reach, origin):
        place = origin + jnp.where(side == 0, -distance, distance)
        inside = (distance >= 0) & (distance < reach) & (place >= 0) & (place < reach)
        return place, inside & jnp.logical_or(distance > 0, side == 0)

    def other_columns(body):
        def one(i, carry):
            yy, valid = visited(i // 2 + 1, lax.rem(i, 2), grid_fast, y)
            @pl.when(valid)
            def _():
                body(yy)
            return carry
        lax.fori_loop(0, 2 * (grid_fast - 1), one, 0)

    def event(e, carry):
        distance = e // (2 * PIECES)
        piece = lax.rem(e // 2, PIECES)
        side = lax.rem(e, 2)

        zz, valid = visited(distance, side, grid_slow, z)
        @pl.when(valid & (distance > 0))
        def _():
            arrived(zz, y, core, piece)
            each((0, 1, 2, 3, 4), (side == 1, side == 0, yes, yes, yes), zz, y, piece, False, start)

        z1, valid1 = visited(distance - 1, side, grid_slow, z)
        @pl.when(valid1 & (piece == 0))
        def _():
            for p in range(PIECES):
                arrived(z1, y, 1 - core, p)
            compute(z1, y)

        z2, valid2 = visited(distance - 2, side, grid_slow, z)
        @pl.when(valid2)
        def _():
            def receive(yy):
                arrived(z2, yy, core, piece)
                each((2, 3, 4), (yy > y, yy < y, yes), z2, yy, piece, False, start)
            other_columns(receive)

        @pl.when(valid2 & (piece == PIECES - 1))
        def _():
            def meet(yy):
                for p in range(PIECES):
                    arrived(z2, yy, 1 - core, p)
                compute(z2, yy)
            other_columns(meet)
        return carry

    lax.fori_loop(0, 2 * PIECES * (grid_slow + 2), event, 0)

    total = row_total[...]
    density = row_max[...] + jnp.log(total)
    dens_ref[...] = jnp.transpose(jnp.broadcast_to(density, (rows, rows)))[:1, :]
    mean_ref[...] = (acc[...] / total).astype(mean_ref.dtype)

    for piece in range(PIECES):
        each((2, 3, 0, 1, 4), (yes,) * 5, z, y, piece, True, finish)

    def drain(e, carry):
        distance = e // (2 * PIECES)
        piece = lax.rem(e // 2, PIECES)
        side = lax.rem(e, 2)
        zz, valid = visited(distance, side, grid_slow, z)
        @pl.when(valid & (distance > 0))
        def _():
            each((0, 1, 2, 3, 4), (side == 1, side == 0, yes, yes, yes), zz, y, piece, False, finish)
        @pl.when(valid)
        def _():
            def sent(yy):
                each((2, 3, 4), (yy > y, yy < y, yes), zz, yy, piece, False, finish)
            other_columns(sent)
        return carry

    lax.fori_loop(0, 2 * PIECES * grid_slow, drain, 0)


def per_device(device_count, embeddings, labels, row_slot):
    rows, width = embeddings.shape
    grid_slow, grid_fast = chip_grid(device_count)
    chips = device_count // CORES
    vmem = pl.BlockSpec(memory_space=pltpu.VMEM)
    density, mean = pl.pallas_call(
        functools.partial(kernel, grid_slow, grid_fast),
        out_shape=(
            jax.ShapeDtypeStruct((1, rows), jnp.float32),
            jax.ShapeDtypeStruct((rows, width), jnp.bfloat16),
        ),
        in_specs=[vmem, vmem],
        out_specs=(vmem, vmem),
        scratch_shapes=[
            pltpu.VMEM((device_count * rows, width), jnp.bfloat16),
            pltpu.VMEM((device_count * PIECES, 1, rows), jnp.int32),
            pltpu.VMEM((rows, width), jnp.float32),
            pltpu.VMEM((rows, 1), jnp.float32),
            pltpu.VMEM((rows, 1), jnp.float32),
            pltpu.SemaphoreType.DMA((5, chips * PIECES)),
            pltpu.SemaphoreType.DMA((device_count * PIECES,)),
            pltpu.SemaphoreType.DMA((5, chips * PIECES)),
            pltpu.SemaphoreType.DMA((device_count * PIECES,)),
            pltpu.SemaphoreType.DMA((2,)),
        ],
        compiler_params=pltpu.CompilerParams(collective_id=0, has_side_effects=True),
    )(embeddings, labels.reshape(1, rows))
    return density.reshape(rows), mean


def solution(mesh):
    return jax.shard_map(
        functools.partial(per_device, mesh.shape["docs"]),
        mesh=mesh,
        in_specs=(P(("groups", "docs"), None), P(("groups", "docs")), P(("groups", "docs"))),
        out_specs=(P(("groups", "docs")), P(("groups", "docs"), None)),
        check_vma=False,
    )
```

time: 77 us -> 39 us (0.51)
  Pallas kernels: 0 us -> 35.5 us
  waiting for transfers between devices: 32.4 us -> 0 us
  blocking collectives: 23.4 us -> 0 us
  between operations: 14 us -> 0.65 us
  matrix products: 5.77 us -> 0 us
  local copies, waits for them, and re-layouts: 0.01 us -> 2.74 us
  other arithmetic: 0.98 us -> 0 us
    pallas_call x0 -> x1, Pallas kernels: none -> 35.5 us  [per_device(): pl.pallas_call(functools.partial(kernel, grid_slow, grid_fast), out_shape...]
    all_gather x1 -> x0, waiting for transfers between devices: 31.7 us -> none  [per_device(): all_x = lax.all_gather(embeddings, 'docs', axis=0, tiled=True)]
    all_gather x1 -> x0, blocking collectives: 23.4 us -> none  [per_device(): all_labels = lax.all_gather(labels, 'docs', axis=0, tiled=True)]
    dot_general x2 -> x0, matrix products: 5.77 us -> none  [the longest x1 4.03 us: per_device(): jnp.dot(embeddings, all_x.T, preferred_element_type=jnp.float32)]
    unnamed x4, local copies, waits for them, and re-layouts: 0.01 us -> 2.74 us
  transfers between devices with their start and end apart: 1 -> 0, of which waited for: 1 -> 0; matrix products, arithmetic and copies ran while one was open for 0% -> 0% of each run, Pallas kernels for 0% -> 0%
where the time goes in v2:
time: 39 us; the launch traced here: 38.9 us
  Pallas kernels  35.5 us (91%)
  local copies, waits for them, and re-layouts  2.74 us (7%)
  between operations  0.65 us (2%)
    pallas_call x1, Pallas kernels, per_device(): pl.pallas_call(functools.partial(kernel, grid_slow, grid_fast), out_shape...  35.5 us
    unnamed x4, local copies, waits for them, and re-layouts  2.74 us

profile of v2, /device:TPU:1, one launch (start us, length us, event | category | flops | bytes accessed | tf_op | source)
XLA Modules:
  0.0 38.9 jit_solution(10518957780761610428)
XLA Ops:
  0.6 35.5 %shard_map.41 = (f32[1,128]{1,0:T(1,128)}, bf16[128,1024]{1,0:T(8,128)(2,1)}) custom-call(bf16[128,1024]{1,0:T(8,128)(2,1)} %x_ref.1, s32[1,128]{1,0:T(1,128)} %bitcast.2), custom_call_target="tpu_custom_call" | custom-call | tf_op jit(solution)/shard_map/pallas_call | solution.py:224
  36.1 0.0 copy-start
  36.1 0.6 %copy-done = f32[1,128]{1,0:T(1,128)S(1)} copy-done((f32[1,128]{1,0:T(1,128)S(1)}, f32[1,128]{1,0:T(1,128)}, u32[]{:S(2)}) %copy-start) | copy-done | bytes 536
  36.7 0.5 %copy.6 = f32[128]{0:T(128)} copy(f32[128]{0:T(128)S(1)} %bitcast.3) | data formatting | bytes 1024
  37.2 1.7 %copy.7 = bf16[128,1024]{1,0:T(8,128)(2,1)} copy(bf16[128,1024]{1,0:T(8,128)(2,1)} %get-tuple-element.9) | data formatting | bytes 524288
Async XLA Ops:
  36.1 0.6 %copy-start = (f32[1,128]{1,0:T(1,128)S(1)}, f32[1,128]{1,0:T(1,128)}, u32[]{:S(2)}) copy-start(f32[1,128]{1,0:T(1,128)} %get-tuple-element.4) | copy-start | bytes 1540

commit v3 on v2

v3 whole, which is shorter than its diff:
```python
import functools
import math

import jax
import jax.numpy as jnp
from jax import lax
from jax.experimental import pallas as pl
from jax.experimental.pallas import tpu as pltpu
from jax.sharding import PartitionSpec as P

MESH = pl.DeviceIdType.MESH
CORES = 2
PIECES = 4
HALVES = 2

neg_large = -1e30
kernel_gain = 4.0


def chip_grid(device_count):
    chips = device_count // CORES
    fast = 1
    while (2 * fast) * (2 * fast) <= chips and chips % (2 * fast) == 0:
        fast *= 2
    return chips // fast, fast


def kernel(
    grid_slow, grid_fast, x_ref, lab_ref, dens_ref, mean_ref,
    buf, labs, mine, acc, row_max, row_total,
    send_sem, recv_sem, lsend_sem, lrecv_sem, own_sem, own_lab_sem,
):
    rows, width = x_ref.shape
    part = rows // PIECES
    group = PIECES // HALVES
    half_rows = rows // HALVES
    keys = CORES * half_rows
    detour = PIECES // 2 if grid_fast == 2 and grid_slow % 2 == 0 else 0
    me = lax.axis_index("docs")
    core = lax.rem(me, CORES)
    chip = me // CORES
    y = lax.rem(chip, grid_fast)
    z = chip // grid_fast
    pair = z + 1 - 2 * lax.rem(z, 2)

    def device(zz, yy, cc):
        return (zz * grid_fast + yy) * CORES + cc

    targets = (
        (z > 0, device(z - 1, y, core)),
        (z < grid_slow - 1, device(z + 1, y, core)),
        (y > 0, device(z, y - 1, core)),
        (y < grid_fast - 1, device(z, y + 1, core)),
        (z >= 0, device(z, y, 1 - core)),
    )

    barrier = pltpu.get_barrier_semaphore()
    for there, target in targets:
        @pl.when(there)
        def _():
            pl.semaphore_signal(barrier, inc=1, device_id={"docs": target}, device_id_type=MESH)

    def data_of(zz, yy, cc, piece):
        where = ((zz * grid_fast + yy) * HALVES + piece // group) * CORES + cc
        return buf.at[pl.ds(pl.multiple_of((where * group + lax.rem(piece, group)) * part, part), part)]

    own_copies = [pltpu.make_async_copy(x_ref, mine, own_sem.at[PIECES])]
    for piece in range(PIECES):
        own_copies.append(
            pltpu.make_async_copy(
                x_ref.at[pl.ds(piece * part, part)], data_of(z, y, core, piece), own_sem.at[piece]
            )
        )
    own_copies.append(pltpu.make_async_copy(lab_ref, labs.at[me], own_lab_sem.at[0]))
    for copy in own_copies:
        copy.start()
    pl.semaphore_wait(barrier, sum(there.astype(jnp.int32) for there, _ in targets))

    def data_copy(direction, zz, yy, piece, own):
        data = data_of(zz, yy, core, piece)
        return pltpu.make_async_remote_copy(
            x_ref.at[pl.ds(piece * part, part)] if own else data, data,
            send_sem.at[direction, (zz * grid_fast + yy) * PIECES + piece],
            recv_sem.at[device(zz, yy, core) * PIECES + piece],
            device_id={"docs": targets[direction][1]}, device_id_type=MESH,
        )

    def lab_copy(direction, zz, yy, own):
        slot = device(zz, yy, core)
        return pltpu.make_async_remote_copy(
            lab_ref if own else labs.at[slot], labs.at[slot],
            lsend_sem.at[direction, zz * grid_fast + yy], lrecv_sem.at[slot],
            device_id={"docs": targets[direction][1]}, device_id_type=MESH,
        )

    def each(directions, wanted, zz, yy, piece, own, act):
        for direction, want in zip(directions, wanted):
            @pl.when(jnp.logical_and(targets[direction][0], want))
            def _():
                @pl.when(piece == 0)
                def _():
                    act(lab_copy(direction, zz, yy, own))
                act(data_copy(direction, zz, yy, piece, own))

    start = lambda copy: copy.start()
    finish = lambda copy: copy.wait_send()

    def arrived(zz, yy, cc, piece):
        slot = device(zz, yy, cc)
        @pl.when(piece == 0)
        def _():
            pltpu.make_async_remote_copy(
                labs.at[slot], labs.at[slot], lsend_sem.at[0, 0], lrecv_sem.at[slot],
                device_id={"docs": targets[4][1]}, device_id_type=MESH,
            ).wait_recv()
        data = data_of(zz, yy, cc, piece)
        pltpu.make_async_remote_copy(
            data, data, send_sem.at[0, 0], recv_sem.at[slot * PIECES + piece],
            device_id={"docs": targets[4][1]}, device_id_type=MESH,
        ).wait_recv()

    yes = z >= 0
    for piece in range(PIECES):
        each((2, 3, 0, 1, 4), (yes,) * 5, z, y, piece, True, start)

    row_max[...] = jnp.full_like(row_max, neg_large)
    row_total[...] = jnp.zeros_like(row_total)
    acc[...] = jnp.zeros_like(acc)
    own_copies[-1].wait()
    label_column = jnp.transpose(
        jnp.broadcast_to(labs[me].astype(jnp.float32), (rows, rows))
    )[:, :1]
    column = lax.broadcasted_iota(jnp.int32, (rows, keys), 1)
    gap = (
        column + (column // half_rows) * (rows - half_rows)
        - lax.broadcasted_iota(jnp.int32, (rows, keys), 0)
    )
    for copy in own_copies[:-1]:
        copy.wait()

    def compute(zz, yy, half):
        where = zz * grid_fast + yy
        values = buf[pl.ds(pl.multiple_of((where * HALVES + half) * keys, keys), keys), :]
        tags = []
        for cc in range(CORES):
            tag = labs[where * CORES + cc].astype(jnp.float32)
            pieces = [tag[:, h * half_rows:(h + 1) * half_rows] for h in range(HALVES)]
            picked = pieces[0]
            for h in range(1, HALVES):
                picked = jnp.where(half == h, pieces[h], picked)
            tags.append(picked)
        tags = jnp.concatenate(tags, axis=1)
        scores = lax.dot_general(
            mine[...], values, (((1,), (1,)), ((), ())), preferred_element_type=jnp.float32
        ) * (kernel_gain / math.sqrt(width))
        self_gap = jnp.where(where == chip, core * rows - half * half_rows, CORES * rows)
        near = (label_column == tags) & (gap != self_gap)
        masked = jnp.where(near, scores, neg_large)
        before = row_max[...]
        peak = jnp.maximum(before, jnp.max(masked, axis=1, keepdims=True))
        weights = jnp.where(near, jnp.exp(masked - peak), 0.0)
        scale = jnp.exp(before - peak)
        row_max[...] = peak
        row_total[...] = row_total[...] * scale + jnp.sum(weights, axis=1, keepdims=True)
        acc[...] = acc[...] * scale + jnp.dot(
            weights.astype(jnp.bfloat16), values, preferred_element_type=jnp.float32
        )

    def meet(zz, yy, half):
        def one(p, carry):
            arrived(zz, yy, 1 - core, half * group + p)
            return carry
        lax.fori_loop(0, group, one, 0)
        compute(zz, yy, half)

    def visited(distance, side, reach, origin):
        place = origin + jnp.where(side == 0, -distance, distance)
        inside = (distance >= 0) & (distance < reach) & (place >= 0) & (place < reach)
        return place, inside & jnp.logical_or(distance > 0, side == 0)

    def other_columns(body):
        if grid_fast == 2:
            body(1 - y)
            return
        def one(i, carry):
            yy, valid = visited(i // 2 + 1, lax.rem(i, 2), grid_fast, y)
            @pl.when(valid)
            def _():
                body(yy)
            return carry
        lax.fori_loop(0, 2 * (grid_fast - 1), one, 0)

    def detoured(zz, piece):
        return (zz == pair) & (piece >= PIECES - detour)

    def along(zz, piece, side, act):
        straight = jnp.logical_not(detoured(zz, piece))
        each((0, 1, 2, 3, 4), (side == 1, side == 0, straight, straight, yes), zz, y, piece, False, act)

    def across(zz, yy, piece, act):
        each((2, 3, 4), (yy > y, yy < y, yes), zz, yy, piece, False, act)

    def to_pair(act):
        for piece in range(PIECES - detour, PIECES):
            each((0, 1), (pair < z, pair > z), z, 1 - y, piece, False, act)

    def receive(zz, yy, piece):
        arrived(zz, yy, core, piece)
        across(zz, yy, piece, start)

    def event(e, carry):
        distance = e // (2 * PIECES)
        piece = lax.rem(e // 2, PIECES)
        side = lax.rem(e, 2)
        half = piece // group

        if detour:
            @pl.when(e == 2 * PIECES * max(3, grid_slow - 1))
            def _():
                to_pair(start)

        zz, valid = visited(distance, side, grid_slow, z)
        @pl.when(valid & (distance > 0))
        def _():
            arrived(zz, y, core, piece)
            along(zz, piece, side, start)

        z1, valid1 = visited(distance - 1, side, grid_slow, z)
        z2, valid2 = visited(distance - 2, side, grid_slow, z)
        valid2 = valid2 & jnp.logical_not(detoured(z2, piece))
        @pl.when(valid2)
        def _():
            other_columns(lambda yy: receive(z2, yy, piece))

        near = valid1 & (lax.rem(piece, group) == 0)
        if grid_fast == 2:
            far = valid2 & (lax.rem(piece, group) == group - 1)
            @pl.when(near | far)
            def _():
                def one(i, carry):
                    @pl.when(jnp.where(i == 0, near, far))
                    def _():
                        meet(jnp.where(i == 0, z1, z2), jnp.where(i == 0, y, 1 - y), half)
                    return carry
                lax.fori_loop(0, 2, one, 0)
        else:
            @pl.when(near)
            def _():
                meet(z1, y, half)
            @pl.when(valid2 & (lax.rem(piece, group) == group - 1))
            def _():
                other_columns(lambda yy: meet(z2, yy, half))
        return carry

    lax.fori_loop(0, 2 * PIECES * max(4, grid_slow + 2), event, 0)
    if detour:
        for piece in range(PIECES - detour, PIECES):
            receive(pair, 1 - y, piece)
        for half in range((PIECES - detour) // group, HALVES):
            meet(pair, 1 - y, half)

    total = row_total[...]
    density = row_max[...] + jnp.log(total)
    dens_ref[...] = jnp.transpose(jnp.broadcast_to(density, (rows, rows)))[:1, :]
    mean_ref[...] = (acc[...] / total).astype(mean_ref.dtype)

    for piece in range(PIECES):
        each((2, 3, 0, 1, 4), (yes,) * 5, z, y, piece, True, finish)
    if detour:
        to_pair(finish)

    def drain(e, carry):
        distance = e // (2 * PIECES)
        piece = lax.rem(e // 2, PIECES)
        side = lax.rem(e, 2)
        zz, valid = visited(distance, side, grid_slow, z)
        @pl.when(valid & (distance > 0))
        def _():
            along(zz, piece, side, finish)
        @pl.when(valid)
        def _():
            other_columns(lambda yy: across(zz, yy, piece, finish))
        return carry

    lax.fori_loop(0, 2 * PIECES * grid_slow, drain, 0)


def per_device(device_count, embeddings, labels, row_slot):
    rows, width = embeddings.shape
    grid_slow, grid_fast = chip_grid(device_count)
    chips = device_count // CORES
    vmem = pl.BlockSpec(memory_space=pltpu.VMEM)
    density, mean = pl.pallas_call(
        functools.partial(kernel, grid_slow, grid_fast),
        out_shape=(
            jax.ShapeDtypeStruct((1, rows), jnp.float32),
            jax.ShapeDtypeStruct((rows, width), jnp.bfloat16),
        ),
        in_specs=[pl.BlockSpec(memory_space=pl.ANY), pl.BlockSpec(memory_space=pl.ANY)],
        out_specs=(vmem, vmem),
        scratch_shapes=[
            pltpu.VMEM((device_count * rows, width), jnp.bfloat16),
            pltpu.VMEM((device_count, 1, rows), jnp.int32),
            pltpu.VMEM((rows, width), jnp.bfloat16),
            pltpu.VMEM((rows, width), jnp.float32),
            pltpu.VMEM((rows, 1), jnp.float32),
            pltpu.VMEM((rows, 1), jnp.float32),
            pltpu.SemaphoreType.DMA((5, chips * PIECES)),
            pltpu.SemaphoreType.DMA((device_count * PIECES,)),
            pltpu.SemaphoreType.DMA((5, chips)),
            pltpu.SemaphoreType.DMA((device_count,)),
            pltpu.SemaphoreType.DMA((PIECES + 1,)),
            pltpu.SemaphoreType.DMA((1,)),
        ],
        compiler_params=pltpu.CompilerParams(collective_id=0, has_side_effects=True),
    )(embeddings, labels.reshape(1, rows))
    return density.reshape(rows), mean


def solution(mesh):
    return jax.shard_map(
        functools.partial(per_device, mesh.shape["docs"]),
        mesh=mesh,
        in_specs=(P(("groups", "docs"), None), P(("groups", "docs")), P(("groups", "docs"))),
        out_specs=(P(("groups", "docs")), P(("groups", "docs"), None)),
        check_vma=False,
    )
```

time: 39 us -> 43.9 us (1.13)
  Pallas kernels: 35.5 us -> 40.3 us
    pallas_call x1, Pallas kernels: 35.5 us -> 40.3 us  [per_device(): pl.pallas_call(functools.partial(kernel, grid_slow, grid_fast), out_shape...]
where the time goes in v3:
time: 43.9 us; the launch traced here: 43.7 us
  Pallas kernels  40.3 us (92%)
  local copies, waits for them, and re-layouts  2.74 us (6%)
  between operations  0.65 us (1%)
    pallas_call x1, Pallas kernels, per_device(): pl.pallas_call(functools.partial(kernel, grid_slow, grid_fast), out_shape...  40.3 us
    unnamed x4, local copies, waits for them, and re-layouts  2.74 us

profile of v3, /device:TPU:1, one launch (start us, length us, event | category | flops | bytes accessed | tf_op | source)
XLA Modules:
  0.0 43.7 jit_solution(12626286333706363531)
XLA Ops:
  0.6 40.3 %shard_map.41 = (f32[1,128]{1,0:T(1,128)}, bf16[128,1024]{1,0:T(8,128)(2,1)}) custom-call(bf16[128,1024]{1,0:T(8,128)(2,1)} %x_ref.1, s32[1,128]{1,0:T(1,128)} %bitcast.2), custom_call_target="tpu_custom_call" | custom-call | tf_op jit(solution)/shard_map/pallas_call | solution.py:293
  40.9 0.0 copy-start
  41.0 0.6 %copy-done = f32[1,128]{1,0:T(1,128)S(1)} copy-done((f32[1,128]{1,0:T(1,128)S(1)}, f32[1,128]{1,0:T(1,128)}, u32[]{:S(2)}) %copy-start) | copy-done | bytes 536
  41.5 0.5 %copy.6 = f32[128]{0:T(128)} copy(f32[128]{0:T(128)S(1)} %bitcast.3) | data formatting | bytes 1024
  42.0 1.7 %copy.7 = bf16[128,1024]{1,0:T(8,128)(2,1)} copy(bf16[128,1024]{1,0:T(8,128)(2,1)} %get-tuple-element.9) | data formatting | bytes 524288
Async XLA Ops:
  40.9 0.6 %copy-start = (f32[1,128]{1,0:T(1,128)S(1)}, f32[1,128]{1,0:T(1,128)}, u32[]{:S(2)}) copy-start(f32[1,128]{1,0:T(1,128)} %get-tuple-element.4) | copy-start | bytes 1540

commit v4 on v3

--- a/solution.py
+++ b/solution.py
@@ -10,8 +10,8 @@
 
 MESH = pl.DeviceIdType.MESH
 CORES = 2
-PIECES = 4
-HALVES = 2
+PIECES = 2
+HALVES = 1
 
 neg_large = -1e30
 kernel_gain = 4.0
@@ -35,7 +35,7 @@
     group = PIECES // HALVES
     half_rows = rows // HALVES
     keys = CORES * half_rows
-    detour = PIECES // 2 if grid_fast == 2 and grid_slow % 2 == 0 else 0
+    detour = 0
     me = lax.axis_index("docs")
     core = lax.rem(me, CORES)
     chip = me // CORES
@@ -293,8 +293,8 @@
     density, mean = pl.pallas_call(
         functools.partial(kernel, grid_slow, grid_fast),
         out_shape=(
-            jax.ShapeDtypeStruct((1, rows), jnp.float32),
-            jax.ShapeDtypeStruct((rows, width), jnp.bfloat16),
+            pltpu.VMEM((1, rows), jnp.float32),
+            pltpu.VMEM((rows, width), jnp.bfloat16),
         ),
         in_specs=[pl.BlockSpec(memory_space=pl.ANY), pl.BlockSpec(memory_space=pl.ANY)],
         out_specs=(vmem, vmem),

time: 43.9 us -> 35.3 us (0.80)
  Pallas kernels: 40.3 us -> 33.3 us
  local copies, waits for them, and re-layouts: 2.74 us -> 1.22 us
    pallas_call x1, Pallas kernels: 40.3 us -> 33.3 us  [per_device(): pl.pallas_call(functools.partial(kernel, grid_slow, grid_fast), out_shape...]
    unnamed x4 -> x2, local copies, waits for them, and re-layouts: 2.74 us -> 1.22 us
where the time goes in v4:
time: 35.3 us; the launch traced here: 35.2 us
  Pallas kernels  33.3 us (94%)
  local copies, waits for them, and re-layouts  1.22 us (3%)
  between operations  0.64 us (2%)
    pallas_call x1, Pallas kernels, per_device(): pl.pallas_call(functools.partial(kernel, grid_slow, grid_fast), out_shape...  33.3 us
    unnamed x2, local copies, waits for them, and re-layouts  1.22 us

profile of v4, /device:TPU:1, one launch (start us, length us, event | category | flops | bytes accessed | tf_op | source)
XLA Modules:
  0.0 35.2 jit_solution(11198462025890879559)
XLA Ops:
  0.6 33.3 %shard_map.41 = (f32[1,128]{1,0:T(1,128)S(1)}, bf16[128,1024]{1,0:T(8,128)(2,1)S(1)}) custom-call(bf16[128,1024]{1,0:T(8,128)(2,1)} %x_ref.1, s32[1,128]{1,0:T(1,128)} %bitcast.3), custom_call_target="tpu_custom_call" | custom-call | tf_op jit(solution)/shard_map/pallas_call | solution.py:293
  34.0 0.5 %copy.6 = f32[128]{0:T(128)} copy(f32[128]{0:T(128)S(1)} %bitcast.2) | data formatting | bytes 1024
  34.5 0.7 %copy.7 = bf16[128,1024]{1,0:T(8,128)(2,1)} copy(bf16[128,1024]{1,0:T(8,128)(2,1)S(1)} %get-tuple-element.7) | data formatting | bytes 524288

commit v5 on v4

--- a/solution.py
+++ b/solution.py
@@ -35,13 +35,11 @@
     group = PIECES // HALVES
     half_rows = rows // HALVES
     keys = CORES * half_rows
-    detour = 0
     me = lax.axis_index("docs")
     core = lax.rem(me, CORES)
     chip = me // CORES
     y = lax.rem(chip, grid_fast)
     z = chip // grid_fast
-    pair = z + 1 - 2 * lax.rem(z, 2)
 
     def device(zz, yy, cc):
         return (zz * grid_fast + yy) * CORES + cc
@@ -190,19 +188,11 @@
             return carry
         lax.fori_loop(0, 2 * (grid_fast - 1), one, 0)
 
-    def detoured(zz, piece):
-        return (zz == pair) & (piece >= PIECES - detour)
-
     def along(zz, piece, side, act):
-        straight = jnp.logical_not(detoured(zz, piece))
-        each((0, 1, 2, 3, 4), (side == 1, side == 0, straight, straight, yes), zz, y, piece, False, act)
+        each((0, 1, 2, 3, 4), (side == 1, side == 0, yes, yes, yes), zz, y, piece, False, act)
 
     def across(zz, yy, piece, act):
         each((2, 3, 4), (yy > y, yy < y, yes), zz, yy, piece, False, act)
-
-    def to_pair(act):
-        for piece in range(PIECES - detour, PIECES):
-            each((0, 1), (pair < z, pair > z), z, 1 - y, piece, False, act)
 
     def receive(zz, yy, piece):
         arrived(zz, yy, core, piece)
@@ -214,10 +204,10 @@
         side = lax.rem(e, 2)
         half = piece // group
 
-        if detour:
-            @pl.when(e == 2 * PIECES * max(3, grid_slow - 1))
-            def _():
-                to_pair(start)
+        @pl.when(e == 2 * PIECES * grid_slow)
+        def _():
+            for p in range(PIECES):
+                each((2, 3, 0, 1, 4), (yes,) * 5, z, y, p, True, finish)
 
         zz, valid = visited(distance, side, grid_slow, z)
         @pl.when(valid & (distance > 0))
@@ -227,10 +217,17 @@
 
         z1, valid1 = visited(distance - 1, side, grid_slow, z)
         z2, valid2 = visited(distance - 2, side, grid_slow, z)
-        valid2 = valid2 & jnp.logical_not(detoured(z2, piece))
         @pl.when(valid2)
         def _():
             other_columns(lambda yy: receive(z2, yy, piece))
+            @pl.when(distance > 2)
+            def _():
+                along(z2, piece, side, finish)
+
+        z3, valid3 = visited(distance - 3, side, grid_slow, z)
+        @pl.when(valid3)
+        def _():
+            other_columns(lambda yy: across(z3, yy, piece, finish))
 
         near = valid1 & (lax.rem(piece, group) == 0)
         if grid_fast == 2:
@@ -252,37 +249,18 @@
                 other_columns(lambda yy: meet(z2, yy, half))
         return carry
 
-    lax.fori_loop(0, 2 * PIECES * max(4, grid_slow + 2), event, 0)
-    if detour:
-        for piece in range(PIECES - detour, PIECES):
-            receive(pair, 1 - y, piece)
-        for half in range((PIECES - detour) // group, HALVES):
-            meet(pair, 1 - y, half)
+    lax.fori_loop(0, 2 * PIECES * (grid_slow + 2), event, 0)
 
     total = row_total[...]
     density = row_max[...] + jnp.log(total)
     dens_ref[...] = jnp.transpose(jnp.broadcast_to(density, (rows, rows)))[:1, :]
     mean_ref[...] = (acc[...] / total).astype(mean_ref.dtype)
 
-    for piece in range(PIECES):
-        each((2, 3, 0, 1, 4), (yes,) * 5, z, y, piece, True, finish)
-    if detour:
-        to_pair(finish)
-
-    def drain(e, carry):
-        distance = e // (2 * PIECES)
-        piece = lax.rem(e // 2, PIECES)
-        side = lax.rem(e, 2)
-        zz, valid = visited(distance, side, grid_slow, z)
-        @pl.when(valid & (distance > 0))
-        def _():
-            along(zz, piece, side, finish)
+    for e in range(2 * PIECES):
+        last, valid = visited(grid_slow - 1, e % 2, grid_slow, z)
         @pl.when(valid)
         def _():
-            other_columns(lambda yy: across(zz, yy, piece, finish))
-        return carry
-
-    lax.fori_loop(0, 2 * PIECES * grid_slow, drain, 0)
+            other_columns(lambda yy: across(last, yy, e // 2, finish))
 
 
 def per_device(device_count, embeddings, labels, row_slot):

time: 35.3 us -> 34.4 us (0.975)
  Pallas kernels: 33.3 us -> 32.4 us
    pallas_call x1, Pallas kernels: 33.3 us -> 32.4 us  [per_device(): pl.pallas_call(functools.partial(kernel, grid_slow, grid_fast), out_shape...]
where the time goes in v5:
time: 34.4 us; the launch traced here: 34.3 us
  Pallas kernels  32.4 us (94%)
  local copies, waits for them, and re-layouts  1.22 us (4%)
  between operations  0.64 us (2%)
    pallas_call x1, Pallas kernels, per_device(): pl.pallas_call(functools.partial(kernel, grid_slow, grid_fast), out_shape...  32.4 us
    unnamed x2, local copies, waits for them, and re-layouts  1.22 us

profile of v5, /device:TPU:1, one launch (start us, length us, event | category | flops | bytes accessed | tf_op | source)
XLA Modules:
  0.0 34.3 jit_solution(13480968525045980039)
XLA Ops:
  0.6 32.4 %shard_map.41 = (f32[1,128]{1,0:T(1,128)S(1)}, bf16[128,1024]{1,0:T(8,128)(2,1)S(1)}) custom-call(bf16[128,1024]{1,0:T(8,128)(2,1)} %x_ref.1, s32[1,128]{1,0:T(1,128)} %bitcast.3), custom_call_target="tpu_custom_call" | custom-call | tf_op jit(solution)/shard_map/pallas_call | solution.py:271
  33.1 0.5 %copy.6 = f32[128]{0:T(128)} copy(f32[128]{0:T(128)S(1)} %bitcast.2) | data formatting | bytes 1024
  33.6 0.7 %copy.7 = bf16[128,1024]{1,0:T(8,128)(2,1)} copy(bf16[128,1024]{1,0:T(8,128)(2,1)S(1)} %get-tuple-element.7) | data formatting | bytes 524288

commit v6 on v5

--- a/solution.py
+++ b/solution.py
@@ -152,7 +152,17 @@
             mine[...], values, (((1,), (1,)), ((), ())), preferred_element_type=jnp.float32
         ) * (kernel_gain / math.sqrt(width))
         self_gap = jnp.where(where == chip, core * rows - half * half_rows, CORES * rows)
-        near = (label_column == tags) & (gap != self_gap)
+        absorb(scores, (label_column == tags) & (gap != self_gap), values)
+
+    def compute_core(zz, yy, cc):
+        slot = device(zz, yy, cc)
+        values = buf[pl.ds(pl.multiple_of(slot * rows, rows), rows), :]
+        scores = lax.dot_general(
+            mine[...], values, (((1,), (1,)), ((), ())), preferred_element_type=jnp.float32
+        ) * (kernel_gain / math.sqrt(width))
+        absorb(scores, label_column == labs[slot].astype(jnp.float32), values)
+
+    def absorb(scores, near, values):
         masked = jnp.where(near, scores, neg_large)
         before = row_max[...]
         peak = jnp.maximum(before, jnp.max(masked, axis=1, keepdims=True))
@@ -189,7 +199,7 @@
         lax.fori_loop(0, 2 * (grid_fast - 1), one, 0)
 
     def along(zz, piece, side, act):
-        each((0, 1, 2, 3, 4), (side == 1, side == 0, yes, yes, yes), zz, y, piece, False, act)
+        each((2, 3, 0, 1, 4), (yes, yes, side == 1, side == 0, yes), zz, y, piece, False, act)
 
     def across(zz, yy, piece, act):
         each((2, 3, 4), (yy > y, yy < y, yes), zz, yy, piece, False, act)
@@ -197,6 +207,8 @@
     def receive(zz, yy, piece):
         arrived(zz, yy, core, piece)
         across(zz, yy, piece, start)
+
+    farthest = jnp.where(2 * z >= grid_slow, 0, grid_slow - 1)
 
     def event(e, carry):
         distance = e // (2 * PIECES)
@@ -231,7 +243,7 @@
 
         near = valid1 & (lax.rem(piece, group) == 0)
         if grid_fast == 2:
-            far = valid2 & (lax.rem(piece, group) == group - 1)
+            far = valid2 & (lax.rem(piece, group) == group - 1) & (z2 != farthest)
             @pl.when(near | far)
             def _():
                 def one(i, carry):
@@ -250,6 +262,16 @@
         return carry
 
     lax.fori_loop(0, 2 * PIECES * (grid_slow + 2), event, 0)
+    if grid_fast == 2:
+        def last_pair(i, carry):
+            cc = jnp.where(i == 0, core, 1 - core)
+            @pl.when(i == 1)
+            def _():
+                for p in range(PIECES):
+                    arrived(farthest, 1 - y, 1 - core, p)
+            compute_core(farthest, 1 - y, cc)
+            return carry
+        lax.fori_loop(0, CORES, last_pair, 0)
 
     total = row_total[...]
     density = row_max[...] + jnp.log(total)

time: 34.4 us -> 34.3 us (level)
  no operation moved by 1% of the time
where the time goes in v6:
time: 34.3 us; the launch traced here: 34.2 us
  Pallas kernels  32.3 us (94%)
  local copies, waits for them, and re-layouts  1.22 us (4%)
  between operations  0.64 us (2%)
    pallas_call x1, Pallas kernels, per_device(): pl.pallas_call(functools.partial(kernel, grid_slow, grid_fast), out_shape...  32.3 us
    unnamed x2, local copies, waits for them, and re-layouts  1.22 us

profile of v6, /device:TPU:1, one launch (start us, length us, event | category | flops | bytes accessed | tf_op | source)
XLA Modules:
  0.0 34.2 jit_solution(16629846970692178385)
XLA Ops:
  0.6 32.3 %shard_map.41 = (f32[1,128]{1,0:T(1,128)S(1)}, bf16[128,1024]{1,0:T(8,128)(2,1)S(1)}) custom-call(bf16[128,1024]{1,0:T(8,128)(2,1)} %x_ref.1, s32[1,128]{1,0:T(1,128)} %bitcast.3), custom_call_target="tpu_custom_call" | custom-call | tf_op jit(solution)/shard_map/pallas_call | solution.py:293
  32.9 0.5 %copy.6 = f32[128]{0:T(128)} copy(f32[128]{0:T(128)S(1)} %bitcast.2) | data formatting | bytes 1024
  33.5 0.7 %copy.7 = bf16[128,1024]{1,0:T(8,128)(2,1)} copy(bf16[128,1024]{1,0:T(8,128)(2,1)S(1)} %get-tuple-element.7) | data formatting | bytes 524288
